TPU v7x, 32 devices: a whole 2x2x4 slice. The times are simulated.
32 devices in a mesh: head: 4 (over y, core), shard: 8 (over z, x).
Axes of the slice: x: 2, y: 2, z: 4, core: 2. Of those that a mesh axis runs over, the one named last changes fastest.
Arguments:
- inputs: bfloat16 [4, 8, 4, 64, 2048], P(None, 'shard', 'head'), may hold values from -6 to 6
- segments: int32 [4, 8, 4, 64], P(None, 'shard'), may hold values from 0 to 2047, as said below
- query_weight: bfloat16 [2048, 256], P(('head', 'shard')), may hold values from -0.125 to 0.125
- key_weight: bfloat16 [2048, 256], P(('head', 'shard')), may hold values from -0.125 to 0.125
- value_weight: bfloat16 [2048, 2048], P(('head', 'shard')), may hold values from -0.125 to 0.125
- project_weight: bfloat16 [2048, 2048], P(('head', 'shard')), may hold values from -1.5 to 1.5
- attend_gain: bfloat16 [2048], P(('head', 'shard')), may hold values from 0.5 to 1.5
- gate_weight: bfloat16 [2048, 5632], P('shard', 'head'), may hold values from -0.125 to 0.125
- up_weight: bfloat16 [2048, 5632], P('shard', 'head'), may hold values from -0.125 to 0.125
- down_weight: bfloat16 [5632, 2048], P('head', 'shard'), may hold values from -0.078125 to 0.078125
- forward_gain: bfloat16 [2048], P(('head', 'shard')), may hold values from 0.5 to 1.5
- upstream: bfloat16 [4, 8, 4, 64, 2048], P(None, 'shard', 'head'), may hold values from -6 to 6
Outputs:
- outputs: bfloat16 [4, 8, 4, 64, 2048], P(None, 'shard', 'head')
- inputs_grad: float32 [4, 8, 4, 64, 2048], P(None, 'shard', 'head')
- query_grad: float32 [2048, 256], P(('head', 'shard'))
- key_grad: float32 [2048, 256], P(('head', 'shard'))
- value_grad: float32 [2048, 2048], P(('head', 'shard'))
- project_grad: float32 [2048, 2048], P(('head', 'shard'))
- attend_grad: float32 [2048], P(('head', 'shard'))
- gate_grad: float32 [2048, 5632], P('shard', 'head')
- up_grad: float32 [2048, 5632], P('shard', 'head')
- down_grad: float32 [5632, 2048], P('head', 'shard')
- forward_grad: float32 [2048], P(('head', 'shard'))
Inputs may be any that keep to these rules, and one draw needn't show every extreme that they name: `segments`: A token's segment number is the position within its sequence of the first token of its document, so the numbers start at 0 and never fall from one token to the next; one of the 4 sequences is a single document, and another ends with a document of one token.
All inputs are finite; a program needn't handle non-finite values.
Results may differ from a plain program's by a relative error of at most 0.017.
Values may be sent and summed in bfloat16 or wider, within the bound.
No kernel may reach another device: no remote copies, remote signals or barrier semaphores. Data moves between devices by JAX's collectives and lax.ppermute only.
A program may use at most 576 MiB of HBM per device.

v0:
```python
import math
import jax
import jax.numpy as jnp
from jax import lax
from jax.sharding import PartitionSpec as P

D = 2048
HEADS = 16
QK = 16
VD = 128
EPS_NORM = 1e-05
HIGH = lax.Precision.HIGHEST


def carried_in(value, axis, combine, identity):
    size, here = (lax.axis_size(axis), lax.axis_index(axis))
    everything = jax.tree.map(lambda part: lax.all_gather(part, axis), value)
    start = jax.tree.map(
        lambda part, zero: jnp.broadcast_to(jnp.asarray(zero, part.dtype), part.shape),
        value,
        identity,
    )

    def carried_turn(k, before):
        reached = k < here
        new = combine(before, jax.tree.map(lambda part: part[k], everything))
        return jax.tree.map(lambda a, b: jnp.where(reached, a, b), new, before)

    return lax.fori_loop(0, size, carried_turn, start)


def prefix(value, axis, combine, identity):
    size, here = (lax.axis_size(axis), lax.axis_index(axis))
    everything = jax.tree.map(
        lambda part, kind: lax.all_gather(part.astype(kind), axis),
        value,
        jax.tree.map(lambda a: jnp.bfloat16 if a.dtype == jnp.float32 else a.dtype, value),
    )
    start = jax.tree.map(
        lambda part, zero: jnp.broadcast_to(jnp.asarray(zero, part.dtype), part.shape),
        value,
        identity,
    )

    def prefix_turn(k, before):
        at = size - 1 - k
        reached = at > here
        new = combine(
            before, jax.tree.map(lambda part, own: part[at].astype(own.dtype), everything, value)
        )
        return jax.tree.map(lambda a, b: jnp.where(reached, a, b), new, before)

    return lax.fori_loop(0, size, prefix_turn, start)


def features(values):
    qk_size = values.shape[-1]
    square = (values[..., :, None] * values[..., None, :]).reshape(
        values.shape[:-1] + (qk_size * qk_size,)
    )
    ones_col = jnp.ones(values.shape[:-1] + (1,), jnp.float32)
    return jnp.concatenate(
        [ones_col, values * qk_size ** (-0.25), square / math.sqrt(2.0 * qk_size)], axis=-1
    )


def features_back(values, grad_feats):
    qk_size = values.shape[-1]
    linear = grad_feats[..., 1 : 1 + qk_size]
    square = grad_feats[..., 1 + qk_size :].reshape(grad_feats.shape[:-1] + (qk_size, qk_size))
    paired = jnp.einsum("...ij,...j->...i", square, values, precision=HIGH) + jnp.einsum(
        "...ji,...j->...i", square, values, precision=HIGH
    )
    return linear * qk_size ** (-0.25) + paired / math.sqrt(2.0 * qk_size)


def normalize(rows_in):
    inverse = lax.rsqrt(jnp.mean(rows_in * rows_in, axis=-1, keepdims=True) + EPS_NORM)
    return (rows_in * inverse, inverse)


def normalize_back(normed, inverse, grad_normed):
    return inverse * (grad_normed - normed * jnp.mean(grad_normed * normed, axis=-1, keepdims=True))


def forward_combine(earlier, latter):
    keep_old = (latter[2] <= earlier[2]).astype(jnp.float32)
    return (
        latter[0] + keep_old[..., None, None, None] * earlier[0],
        latter[1] + keep_old[..., None, None] * earlier[1],
        jnp.maximum(earlier[2], latter[2]),
    )


def backward_combine(earlier, latter):
    keep_old = (earlier[2] <= latter[2]).astype(jnp.float32)
    return (
        latter[0] + keep_old[..., None, None, None] * earlier[0],
        latter[1] + keep_old[..., None, None] * earlier[1],
        jnp.minimum(earlier[2], latter[2]),
    )


def product(left, right):
    return jnp.dot(left, right, preferred_element_type=jnp.float32)


def contract(pattern, left, right):
    return jnp.einsum(pattern, left, right, precision=HIGH)


def swiglu_pass(active_rows, grad_rows, gate_mat, up_mat, down_mat):
    gate_pre = product(active_rows, gate_mat)
    up_pre = product(active_rows, up_mat)
    sigmoid_gate = jax.nn.sigmoid(gate_pre)
    silu_gate = gate_pre * sigmoid_gate
    hidden_act = (silu_gate * up_pre).astype(jnp.bfloat16)
    down_out = product(hidden_act, down_mat)
    grad_hidden = product(grad_rows, down_mat.T)
    grad_gate = (
        grad_hidden * up_pre * (sigmoid_gate * (1.0 + gate_pre * (1.0 - sigmoid_gate)))
    ).astype(jnp.bfloat16)
    grad_up = (grad_hidden * silu_gate).astype(jnp.bfloat16)
    down_sum = product(hidden_act.T, grad_rows)
    gate_sum = product(active_rows.T, grad_gate)
    up_sum = product(active_rows.T, grad_up)
    grad_active = product(grad_gate, gate_mat.T) + product(grad_up, up_mat.T)
    return (down_out, grad_active, gate_sum, up_sum, down_sum)


def body(
    inputs,
    segments,
    query_weight,
    key_weight,
    value_weight,
    project_weight,
    attend_gain,
    gate_weight,
    up_weight,
    down_weight,
    forward_gain,
    upstream,
):
    groups = lax.axis_size("head")
    per_group = HEADS // groups
    seq_count = inputs.shape[0]
    sub_rows = inputs.shape[3]
    block_len = groups * sub_rows
    token_rows = seq_count * sub_rows
    root_qk = math.sqrt(QK)
    attend_set = (
        lax.all_gather(query_weight, ("head", "shard"), axis=0, tiled=True),
        lax.all_gather(key_weight, ("head", "shard"), axis=0, tiled=True),
        lax.all_gather(value_weight, ("head", "shard"), axis=0, tiled=True),
        lax.all_gather(project_weight, ("head", "shard"), axis=0, tiled=True),
        lax.all_gather(attend_gain, ("head", "shard"), axis=0, tiled=True),
        lax.all_gather(forward_gain, ("head", "shard"), axis=0, tiled=True),
    )
    full_query, full_key, full_value, full_project, full_gain_one, full_gain_two = attend_set
    hidden_in = inputs.reshape(token_rows, D).astype(jnp.float32)
    normed_one, inverse_one = normalize(hidden_in)
    gain_one = full_gain_one.astype(jnp.float32)
    active_one = (normed_one * gain_one).astype(jnp.bfloat16)
    query_rows = product(active_one, full_query).astype(jnp.bfloat16)
    key_rows = product(active_one, full_key).astype(jnp.bfloat16)
    value_rows = product(active_one, full_value).astype(jnp.bfloat16)

    def to_groups(rows_in):
        return rows_in.reshape(seq_count, 1, 1, sub_rows, rows_in.shape[-1])

    def to_heads(shards, head_size):
        return (
            shards.reshape(seq_count, block_len, per_group, head_size)
            .transpose(0, 2, 1, 3)
            .astype(jnp.float32)
        )

    def from_heads(head_arr):
        return (
            head_arr.astype(jnp.bfloat16)
            .transpose(0, 2, 1, 3)
            .reshape(seq_count, 1, groups, sub_rows, per_group * head_arr.shape[-1])
        )

    query_parts, key_parts, value_parts = (
        lax.all_to_all(to_groups(query_rows), "head", split_axis=4, concat_axis=2, tiled=True),
        lax.all_to_all(to_groups(key_rows), "head", split_axis=4, concat_axis=2, tiled=True),
        lax.all_to_all(to_groups(value_rows), "head", split_axis=4, concat_axis=2, tiled=True),
    )
    query_head = to_heads(query_parts, QK)
    key_head = to_heads(key_parts, QK)
    value_head = to_heads(value_parts, VD)
    seg_float = segments.reshape(seq_count, block_len).astype(jnp.float32)
    causal = lax.broadcasted_iota(jnp.int32, (block_len, block_len), 0) >= lax.broadcasted_iota(
        jnp.int32, (block_len, block_len), 1
    )
    visible = (causal[None] & (seg_float[:, :, None] == seg_float[:, None, :])).astype(jnp.float32)[
        :, None
    ]
    scores = contract("bhtd,bhsd->bhts", query_head, key_head) / root_qk
    weights = (1.0 + scores + 0.5 * scores * scores) * visible
    feat_query = features(query_head)
    feat_key = features(key_head)
    last_seg = seg_float[:, -1]
    last_mask = (seg_float == last_seg[:, None]).astype(jnp.float32)[:, None, :, None]
    masked_key = feat_key * last_mask
    state_local = contract("bhtf,bhtc->bhfc", masked_key, value_head)
    norm_local = jnp.sum(masked_key, axis=2)
    start_state = (
        jnp.zeros_like(state_local),
        jnp.zeros_like(norm_local),
        jnp.full_like(last_seg, -1.0),
    )
    state_in, norm_in, last_in = carried_in(
        (state_local, norm_local, last_seg), "shard", forward_combine, start_state
    )
    use_in = (seg_float == last_in[:, None]).astype(jnp.float32)[:, None, :, None]
    numerator = contract("bhts,bhsc->bhtc", weights, value_head) + use_in * contract(
        "bhtf,bhfc->bhtc", feat_query, state_in
    )
    denominator = jnp.sum(weights, axis=-1) + use_in[..., 0] * contract(
        "bhtf,bhf->bht", feat_query, norm_in
    )
    attended = numerator / denominator[..., None]
    mixed_rows = lax.all_to_all(
        from_heads(attended), "head", split_axis=2, concat_axis=4, tiled=True
    ).reshape(token_rows, HEADS * VD)
    attend_out = product(mixed_rows, full_project)
    residual = hidden_in + attend_out
    rows_gate, rows_up, rows_down = (
        lax.all_gather(gate_weight, "shard", axis=0, tiled=True),
        lax.all_gather(up_weight, "shard", axis=0, tiled=True),
        lax.all_gather(down_weight, "shard", axis=1, tiled=True),
    )
    normed_two, inverse_two = normalize(residual)
    gain_two = full_gain_two.astype(jnp.float32)
    active_two = (normed_two * gain_two).astype(jnp.bfloat16)
    grad_out = upstream.reshape(token_rows, D)
    full_gate, full_up, full_down = (
        lax.all_gather(rows_gate, "head", axis=1, tiled=True),
        lax.all_gather(rows_up, "head", axis=1, tiled=True),
        lax.all_gather(rows_down, "head", axis=0, tiled=True),
    )
    down_out, grad_active_two, gate_whole, up_whole, down_whole = swiglu_pass(
        active_two, grad_out, full_gate, full_up, full_down
    )
    gate_part, up_part, down_part = (
        lax.psum_scatter(
            gate_whole.astype(jnp.bfloat16), "head", scatter_dimension=1, tiled=True
        ).astype(jnp.float32),
        lax.psum_scatter(
            up_whole.astype(jnp.bfloat16), "head", scatter_dimension=1, tiled=True
        ).astype(jnp.float32),
        lax.psum_scatter(
            down_whole.astype(jnp.bfloat16), "head", scatter_dimension=0, tiled=True
        ).astype(jnp.float32),
    )
    result = residual + down_out
    outputs = result.astype(jnp.bfloat16).reshape(inputs.shape)
    gate_grad, up_grad, down_grad = (
        lax.psum_scatter(
            gate_part.astype(jnp.bfloat16), "shard", scatter_dimension=0, tiled=True
        ).astype(jnp.float32),
        lax.psum_scatter(
            up_part.astype(jnp.bfloat16), "shard", scatter_dimension=0, tiled=True
        ).astype(jnp.float32),
        lax.psum_scatter(
            down_part.astype(jnp.bfloat16), "shard", scatter_dimension=1, tiled=True
        ).astype(jnp.float32),
    )
    gain_two_sum = jnp.sum(grad_active_two * normed_two, axis=0)
    grad_resid = grad_out.astype(jnp.float32) + normalize_back(
        normed_two, inverse_two, grad_active_two * gain_two
    )
    grad_attend = grad_resid.astype(jnp.bfloat16)
    project_sum = product(mixed_rows.T, grad_attend)
    grad_mixed = product(grad_attend, full_project.T).astype(jnp.bfloat16)
    grad_parts = lax.all_to_all(
        to_groups(grad_mixed), "head", split_axis=4, concat_axis=2, tiled=True
    )
    grad_head = to_heads(grad_parts, VD)
    grad_numer = grad_head / denominator[..., None]
    grad_denom = -jnp.sum(grad_head * attended, axis=-1) / denominator
    grad_value = contract("bhts,bhtc->bhsc", weights, grad_numer)
    grad_weights = contract("bhtc,bhsc->bhts", grad_numer, value_head) + grad_denom[..., None]
    grad_scores = grad_weights * (1.0 + scores) * visible
    grad_query = contract("bhts,bhsd->bhtd", grad_scores, key_head) / root_qk
    grad_key = contract("bhts,bhtd->bhsd", grad_scores, query_head) / root_qk
    grad_feat_query = use_in * (
        contract("bhtc,bhfc->bhtf", grad_numer, state_in)
        + grad_denom[..., None] * norm_in[:, :, None, :]
    )
    grad_state_in = contract("bhtf,bhtc->bhfc", feat_query, use_in * grad_numer)
    grad_norm_in = contract("bhtf,bht->bhf", feat_query, use_in[..., 0] * grad_denom)
    end_state = (
        jnp.zeros_like(grad_state_in),
        jnp.zeros_like(grad_norm_in),
        jnp.full_like(last_in, 1000000000.0),
    )
    grad_state_out, grad_norm_out, unused_keys = prefix(
        (grad_state_in, grad_norm_in, last_in), "shard", backward_combine, end_state
    )
    grad_feat_key = last_mask * (
        contract("bhfc,bhtc->bhtf", grad_state_out, value_head) + grad_norm_out[:, :, None, :]
    )
    grad_value = grad_value + last_mask * contract("bhtf,bhfc->bhtc", feat_key, grad_state_out)
    grad_query = grad_query + features_back(query_head, grad_feat_query)
    grad_key = grad_key + features_back(key_head, grad_feat_key)
    query_back, key_back, value_back = (
        lax.all_to_all(from_heads(grad_query), "head", split_axis=2, concat_axis=4, tiled=True),
        lax.all_to_all(from_heads(grad_key), "head", split_axis=2, concat_axis=4, tiled=True),
        lax.all_to_all(from_heads(grad_value), "head", split_axis=2, concat_axis=4, tiled=True),
    )
    query_back = query_back.reshape(token_rows, HEADS * QK)
    key_back = key_back.reshape(token_rows, HEADS * QK)
    value_back = value_back.reshape(token_rows, HEADS * VD)
    query_sum = product(active_one.T, query_back)
    key_sum = product(active_one.T, key_back)
    value_sum = product(active_one.T, value_back)
    grad_active_one = (
        product(query_back, full_query.T)
        + product(key_back, full_key.T)
        + product(value_back, full_value.T)
    )
    gain_one_sum = jnp.sum(grad_active_one * normed_one, axis=0)
    query_grad, key_grad, value_grad, project_grad, attend_grad, forward_grad = (
        lax.psum_scatter(query_sum, ("head", "shard"), scatter_dimension=0, tiled=True),
        lax.psum_scatter(key_sum, ("head", "shard"), scatter_dimension=0, tiled=True),
        lax.psum_scatter(value_sum, ("head", "shard"), scatter_dimension=0, tiled=True),
        lax.psum_scatter(project_sum, ("head", "shard"), scatter_dimension=0, tiled=True),
        lax.psum_scatter(gain_one_sum, ("head", "shard"), scatter_dimension=0, tiled=True),
        lax.psum_scatter(gain_two_sum, ("head", "shard"), scatter_dimension=0, tiled=True),
    )
    inputs_grad = (
        grad_resid + normalize_back(normed_one, inverse_one, grad_active_one * gain_one)
    ).reshape(inputs.shape)
    return (
        outputs,
        inputs_grad,
        query_grad,
        key_grad,
        value_grad,
        project_grad,
        attend_grad,
        gate_grad,
        up_grad,
        down_grad,
        forward_grad,
    )


def solution(mesh):
    in_specs = (
        P(None, "shard", "head", None, None),
        P(None, "shard", None, None),
        P(("head", "shard"), None),
        P(("head", "shard"), None),
        P(("head", "shard"), None),
        P(("head", "shard"), None),
        P(("head", "shard")),
        P("shard", "head"),
        P("shard", "head"),
        P("head", "shard"),
        P(("head", "shard")),
        P(None, "shard", "head", None, None),
    )
    out_specs = (
        P(None, "shard", "head", None, None),
        P(None, "shard", "head", None, None),
        P(("head", "shard"), None),
        P(("head", "shard"), None),
        P(("head", "shard"), None),
        P(("head", "shard"), None),
        P(("head", "shard")),
        P("shard", "head"),
        P("shard", "head"),
        P("head", "shard"),
        P(("head", "shard")),
    )
    return jax.shard_map(body, mesh=mesh, in_specs=in_specs, out_specs=out_specs, check_vma=False)
```

profile of v0, /device:TPU:0, one launch (start us, length us, event | category | flops | bytes accessed | tf_op | source)
XLA Modules:
  0.0 3412.9 jit_solution(4737021666080043786)
XLA Ops:
  12.9 42.1 %all-reduce.7 = (bf16[2048]{0:T(1024)(128)(2,1)S(1)}, bf16[2048]{0:T(1024)(128)(2,1)S(1)}) all-reduce(bf16[2048]{0:T(1024)(128)(2,1)S(1)} %dynamic-update-slice, bf16[2048]{0:T(1024)(128)(2,1)S(1)} %dynamic-update-slice.2), channel_id=1, replica_groups=mesh['head'=4,'shard'=8] {'head','shard'}, use_global_device_ids=true, to_apply=%add | all-reduce | flops 4096 | bytes 16384
  78.9 68.0 %all-gather.23.cloned.1.call-done = bf16[2048,2048]{1,0:T(8,128)(2,1)} async-done(((bf16[64,2048]{1,0:T(8,128)(2,1)}), bf16[2048,2048]{1,0:T(8,128)(2,1)}) %all-gather.23.cloned.1.call-update) | async-done | bytes 8388624 | tf_op jit(solution)/shard_map/all_gather | solution.py:155
  205.7 34.7 %all-gather.27.cloned.1.call-done = bf16[2048,1408]{1,0:T(8,128)(2,1)} async-done(((bf16[256,1408]{1,0:T(8,128)(2,1)}), bf16[2048,1408]{1,0:T(8,128)(2,1)}) %all-gather.27.cloned.1.call-update) | async-done | bytes 5767184 | tf_op jit(solution)/shard_map/all_gather | solution.py:232
  240.5 92.8 %all-gather.31.cloned.1.call-done = bf16[2048,1408]{1,0:T(8,128)(2,1)} async-done(((bf16[256,1408]{1,0:T(8,128)(2,1)}), bf16[2048,1408]{1,0:T(8,128)(2,1)}) %all-gather.31.cloned.1.call-update) | async-done | bytes 5767184 | tf_op jit(solution)/shard_map/all_gather | solution.py:233
  333.4 93.6 %all-gather.35.cloned.1.call-done = bf16[1408,2048]{1,0:T(8,128)(2,1)} async-done(((bf16[1408,256]{1,0:T(8,128)(2,1)}), bf16[1408,2048]{1,0:T(8,128)(2,1)}) %all-gather.35.cloned.1.call-update) | async-done | bytes 5767184 | tf_op jit(solution)/shard_map/all_gather | solution.py:234
  429.5 52.3 %all-gather.19.cloned.1.call-done = bf16[2048,256]{1,0:T(8,128)(2,1)} async-done(((bf16[64,256]{1,0:T(8,128)(2,1)}), bf16[2048,256]{1,0:T(8,128)(2,1)}) %all-gather.19.cloned.1.call-update) | async-done | bytes 1048592 | tf_op jit(solution)/shard_map/all_gather | solution.py:153
  488.1 39.4 %all-reduce.1 = f32[32]{0:T(128)S(1)} all-reduce(f32[32]{0:T(128)S(1)} %bitcast_dynamic-update-slice_fusion), channel_id=3, replica_groups=mesh['head'=4,'shard'=8] {'shard'}, use_global_device_ids=true, to_apply=%add.1 | all-reduce | flops 32 | bytes 256
  534.9 39.2 %all-gather.2 = f32[32,4,273]{2,1,0:T(4,128)} all-gather(f32[4,4,273]{2,1,0:T(4,128)S(1)} %multiply_reduce_fusion), channel_id=4, replica_groups=mesh['head'=4,'shard'=8] {'shard'}, dimensions={0}, use_global_device_ids=true | all-gather | bytes 157248 | tf_op jit(solution)/shard_map/all_gather | solution.py:17
  584.6 246.1 %all-gather.39.cloned.1.call-done = f32[32,4,273,128]{3,1,2,0:T(4,128)} async-done(((f32[4,4,273,128]{3,1,2,0:T(4,128)}), f32[32,4,273,128]{3,1,2,0:T(4,128)}) %all-gather.39.cloned.1.call-update) | async-done | bytes 17891344 | tf_op jit(solution)/shard_map/all_gather | solution.py:17
  830.7 29.9 while.38
  885.2 24.2 all-to-all-done.3
  926.9 138.3 %all-gather.29.cloned.1.call-done = bf16[2048,5632]{1,0:T(8,128)(2,1)} async-done(((bf16[2048,1408]{1,0:T(8,128)(2,1)}), bf16[2048,5632]{1,0:T(8,128)(2,1)}) %all-gather.29.cloned.1.call-update) | async-done | bytes 23068688 | tf_op jit(solution)/shard_map/all_gather | solution.py:241
  1079.8 130.0 %all-gather.33.cloned.1.call-done = bf16[2048,5632]{1,0:T(8,128)(2,1)} async-done(((bf16[2048,1408]{1,0:T(8,128)(2,1)}), bf16[2048,5632]{1,0:T(8,128)(2,1)}) %all-gather.33.cloned.1.call-update) | async-done | bytes 23068688 | tf_op jit(solution)/shard_map/all_gather | solution.py:242
  1224.0 130.5 %all-gather.37.cloned.1.call-done = bf16[5632,2048]{1,0:T(8,128)(2,1)} async-done(((bf16[1408,2048]{1,0:T(8,128)(2,1)}), bf16[5632,2048]{1,0:T(8,128)(2,1)}) %all-gather.37.cloned.1.call-update) | async-done | bytes 23068688 | tf_op jit(solution)/shard_map/all_gather | solution.py:243
  1384.6 30.6 copy.215
  1415.3 17.6 convolution_convert_fusion.1
  1432.9 30.1 copy.217
  1516.2 29.6 all_to_all.114
  1568.5 24.9 reduce-scatter.31.cloned.1.call-done
  1601.8 161.2 %reduce-scatter.33.cloned.1.call-done = bf16[1408,2048]{1,0:T(8,128)(2,1)} async-done(((bf16[5632,2048]{1,0:T(8,128)(2,1)}), bf16[1408,2048]{1,0:T(8,128)(2,1)}) %reduce-scatter.33.cloned.1.call-update) | async-done | bytes 5767184
  1771.4 160.8 %reduce-scatter.27.cloned.1.call-done = bf16[1408,2048]{1,0:T(8,128)(2,1)} async-done(((bf16[5632,2048]{1,0:T(8,128)(2,1)}), bf16[1408,2048]{1,0:T(8,128)(2,1)}) %reduce-scatter.27.cloned.1.call-update) | async-done | bytes 5767184 | tf_op jit(solution)/shard_map/reduce_scatter | solution.py:255
  1933.9 21.9 all-reduce.3
  1991.1 33.3 all-gather.5
  2030.2 38.9 %all-gather.41.cloned.1.call-done = bf16[32,4,273,128]{3,1,2,0:T(4,128)(2,1)} async-done(((bf16[4,4,273,128]{3,1,2,0:T(4,128)(2,1)}), bf16[32,4,273,128]{3,1,2,0:T(4,128)(2,1)}) %all-gather.41.cloned.1.call-update) | async-done | bytes 8945680 | tf_op jit(solution)/shard_map/all_gather | solution.py:35
  2069.1 28.2 while.39
  2204.4 41.0 %all-reduce.6 = (f32[2048]{0:T(1024)S(1)}, f32[2048]{0:T(1024)S(1)}) all-reduce(f32[2048]{0:T(1024)S(1)} %get-tuple-element.499, f32[2048]{0:T(1024)S(1)} %get-tuple-element.497), channel_id=12, replica_groups=mesh['head'=4,'shard'=8] {'head','shard'}, use_global_device_ids=true, to_apply=%region_16.17.clone | all-reduce | flops 4096 | bytes 32768
  2252.4 44.2 %reduce-scatter.25.cloned.1.call-done = bf16[256,1408]{1,0:T(8,128)(2,1)} async-done(((bf16[2048,1408]{1,0:T(8,128)(2,1)}), bf16[256,1408]{1,0:T(8,128)(2,1)}) %reduce-scatter.25.cloned.1.call-update) | async-done | bytes 720912 | tf_op jit(solution)/shard_map/reduce_scatter | solution.py:265
  2298.8 111.9 %reduce-scatter.29.cloned.1.call-done = bf16[1408,256]{1,0:T(8,128)(2,1)} async-done(((bf16[1408,2048]{1,0:T(8,128)(2,1)}), bf16[1408,256]{1,0:T(8,128)(2,1)}) %reduce-scatter.29.cloned.1.call-update) | async-done | bytes 720912 | tf_op jit(solution)/shard_map/reduce_scatter | solution.py:268
  2413.0 138.0 %reduce-scatter.15.cloned.1.call-done = f32[64,256]{1,0:T(8,128)} async-done(((f32[2048,256]{1,0:T(8,128)}), f32[64,256]{1,0:T(8,128)}) %reduce-scatter.15.cloned.1.call-update) | async-done | bytes 65552 | tf_op jit(solution)/shard_map/reduce_scatter | solution.py:328
  2551.1 137.0 %reduce-scatter.17.cloned.1.call-done = f32[64,256]{1,0:T(8,128)} async-done(((f32[2048,256]{1,0:T(8,128)}), f32[64,256]{1,0:T(8,128)}) %reduce-scatter.17.cloned.1.call-update) | async-done | bytes 65552 | tf_op jit(solution)/shard_map/reduce_scatter | solution.py:329
  2688.1 357.4 %reduce-scatter.21.cloned.1.call-done = f32[64,2048]{1,0:T(8,128)} async-done(((f32[2048,2048]{1,0:T(8,128)}), f32[64,2048]{1,0:T(8,128)}) %reduce-scatter.21.cloned.1.call-update) | async-done | bytes 524304 | tf_op jit(solution)/shard_map/reduce_scatter | solution.py:331
  3045.5 360.4 %reduce-scatter.19.cloned.1.call-done = f32[64,2048]{1,0:T(8,128)} async-done(((f32[2048,2048]{1,0:T(8,128)}), f32[64,2048]{1,0:T(8,128)}) %reduce-scatter.19.cloned.1.call-update) | async-done | bytes 524304 | tf_op jit(solution)/shard_map/reduce_scatter | solution.py:330
  (412 shorter events, 525.6 us)
Async XLA Ops:
  7.2 60.4 %all-gather.21.cloned.1.call-start = ((), (), s32[]{:S(2)}) async-start(), calls=%async_computation.19 | async-start | bytes 1081344 | tf_op jit(solution)/shard_map/all_gather | solution.py:154
  7.9 139.1 %all-gather.23.cloned.1.call-start = ((), (), s32[]{:S(2)}) async-start(), calls=%async_computation.20 | async-start | bytes 8650752 | tf_op jit(solution)/shard_map/all_gather | solution.py:155
  8.7 231.8 %all-gather.27.cloned.1.call-start = ((), (), s32[]{:S(2)}) async-start(), calls=%async_computation.22 | async-start | bytes 6488064 | tf_op jit(solution)/shard_map/all_gather | solution.py:232
  9.4 323.9 %all-gather.31.cloned.1.call-start = ((), (), s32[]{:S(2)}) async-start(), calls=%async_computation.24 | async-start | bytes 6488064 | tf_op jit(solution)/shard_map/all_gather | solution.py:233
  10.0 417.0 %all-gather.35.cloned.1.call-start = ((), (), s32[]{:S(2)}) async-start(), calls=%async_computation.26 | async-start | bytes 6488064 | tf_op jit(solution)/shard_map/all_gather | solution.py:234
  10.6 471.3 %all-gather.19.cloned.1.call-start = ((), (), s32[]{:S(2)}) async-start(), calls=%async_computation.18 | async-start | bytes 1081344 | tf_op jit(solution)/shard_map/all_gather | solution.py:153
  70.3 7.9 all-to-all-start.1
  73.8 457.8 %copy-start.52 = (f32[4,256]{1,0:T(4,128)}, f32[4,256]{1,0:T(4,128)S(1)}, u32[]{:S(2)}) copy-start(f32[4,256]{1,0:T(4,128)S(1)} %compare_convert_fusion.3) | copy-start | bytes 12292
  73.8 793.6 %copy-start.58 = (f32[273]{0:T(512)}, f32[273]{0:T(512)S(1)}, u32[]{:S(2)}) copy-start(f32[273]{0:T(512)S(1)} %pad.3.clone) | copy-start | bytes 3280
  162.1 18.8 all-to-all-start.2
  166.4 664.4 %all-gather.39.cloned.1.call-start = ((), (), s32[]{:S(2)}) async-start(), calls=%async_computation.36 | async-start | bytes 20127744 | tf_op jit(solution)/shard_map/all_gather | solution.py:17
  204.9 715.5 %all-gather.25.cloned.1.call-start = ((), (), s32[]{:S(2)}) async-start(), calls=%async_computation.21 | async-start | bytes 8650752 | tf_op jit(solution)/shard_map/all_gather | solution.py:156
  205.7 859.5 %all-gather.29.cloned.1.call-start = ((), (), s32[]{:S(2)}) async-start(), calls=%async_computation.23 | async-start | bytes 28835840 | tf_op jit(solution)/shard_map/all_gather | solution.py:241
  240.5 969.3 %all-gather.33.cloned.1.call-start = ((), (), s32[]{:S(2)}) async-start(), calls=%async_computation.25 | async-start | bytes 28835840 | tf_op jit(solution)/shard_map/all_gather | solution.py:242
  333.4 1021.2 %all-gather.37.cloned.1.call-start = ((), (), s32[]{:S(2)}) async-start(), calls=%async_computation.27 | async-start | bytes 28835840 | tf_op jit(solution)/shard_map/all_gather | solution.py:243
  484.6 42.9 %all-to-all-start = ((bf16[4,2,8192]{2,1,0:T(2,128)(2,1)}), bf16[4,2,8192]{2,1,0:T(2,128)(2,1)S(1)}, u32[]{:S(2)}, u32[]{:S(2)}) async-start(bf16[4,2,8192]{2,1,0:T(2,128)(2,1)} %reshape.352), calls=%async_computation | async-start | bytes 262144 | tf_op jit(solution)/shard_map/all_to_all | solution.py:187
  881.6 27.8 all-to-all-start.3
  885.1 708.3 %reduce-scatter.31.cloned.1.call-start = ((), (), s32[]{:S(2)}) async-start(), calls=%async_computation.38 | async-start | bytes 28835840
  926.6 577.5 %copy-start.14 = (f32[256,2048]{1,0:T(8,128)}, f32[256,2048]{1,0:T(8,128)S(1)}, u32[]{:S(2)}) copy-start(f32[256,2048]{1,0:T(8,128)S(1)} %get-tuple-element.551) | copy-start | bytes 6291460
  1415.2 347.7 %reduce-scatter.33.cloned.1.call-start = ((), (), s32[]{:S(2)}) async-start(), calls=%async_computation.39 | async-start | bytes 28835840
  1463.0 469.2 %reduce-scatter.27.cloned.1.call-start = ((), (), s32[]{:S(2)}) async-start(), calls=%async_computation.34 | async-start | bytes 28835840 | tf_op jit(solution)/shard_map/reduce_scatter | solution.py:255
  1477.3 591.7 %all-gather.41.cloned.1.call-start = ((), (), s32[]{:S(2)}) async-start(), calls=%async_computation.37 | async-start | bytes 10063872 | tf_op jit(solution)/shard_map/all_gather | solution.py:35
  1568.4 681.6 %reduce-scatter.23.cloned.1.call-start = ((), (), s32[]{:S(2)}) async-start(), calls=%async_computation.32 | async-start | bytes 6488064 | tf_op jit(solution)/shard_map/reduce_scatter | solution.py:262
  1601.7 694.8 %reduce-scatter.25.cloned.1.call-start = ((), (), s32[]{:S(2)}) async-start(), calls=%async_computation.33 | async-start | bytes 6488064 | tf_op jit(solution)/shard_map/reduce_scatter | solution.py:265
  1771.4 160.9 %copy-start.3 = (bf16[4,1,1,64,2048]{4,3,2,1,0:T(8,128)(2,1)S(1)}, bf16[4,1,1,64,2048]{4,3,2,1,0:T(8,128)(2,1)}, u32[]{:S(2)}) copy-start(bf16[4,1,1,64,2048]{4,3,2,1,0:T(8,128)(2,1)} %param.16) | copy-start | bytes 3145732
  1771.4 162.3 %copy-start.55 = (f32[4]{0:T(128)S(1)}, f32[4]{0:T(128)}, u32[]{:S(2)}) copy-start(f32[4]{0:T(128)} %copy-done.54) | copy-start | bytes 52
  1771.4 639.3 %reduce-scatter.29.cloned.1.call-start = ((), (), s32[]{:S(2)}) async-start(), calls=%async_computation.35 | async-start | bytes 6488064 | tf_op jit(solution)/shard_map/reduce_scatter | solution.py:268
  1980.7 43.7 %all-to-all-start.5 = ((bf16[4,2,8192]{2,1,0:T(2,128)(2,1)}), bf16[4,2,8192]{2,1,0:T(2,128)(2,1)S(1)}, u32[]{:S(2)}, u32[]{:S(2)}) async-start(bf16[4,2,8192]{2,1,0:T(2,128)(2,1)} %reshape.356), calls=%async_computation.5 | async-start | bytes 262144 | tf_op jit(solution)/shard_map/all_to_all | solution.py:311
  1984.0 567.1 %reduce-scatter.15.cloned.1.call-start = ((), (), s32[]{:S(2)}) async-start(), calls=%async_computation.28 | async-start | bytes 2162688 | tf_op jit(solution)/shard_map/reduce_scatter | solution.py:328
  2030.2 657.9 %reduce-scatter.17.cloned.1.call-start = ((), (), s32[]{:S(2)}) async-start(), calls=%async_computation.29 | async-start | bytes 2162688 | tf_op jit(solution)/shard_map/reduce_scatter | solution.py:329
  2125.3 920.2 %reduce-scatter.21.cloned.1.call-start = ((), (), s32[]{:S(2)}) async-start(), calls=%async_computation.31 | async-start | bytes 17301504 | tf_op jit(solution)/shard_map/reduce_scatter | solution.py:331
  2135.4 1270.5 %reduce-scatter.19.cloned.1.call-start = ((), (), s32[]{:S(2)}) async-start(), calls=%async_computation.30 | async-start | bytes 17301504 | tf_op jit(solution)/shard_map/reduce_scatter | solution.py:330
  (60 other events, 1331.4 us)
Sparse Core Ops, SparseCore 0:
  11.0 56.5 all-gather.20
  70.6 76.3 all-gather.22
  149.2 91.2 all-gather.26
  242.5 90.8 all-gather.30
  335.2 91.7 all-gather.34
  429.9 51.9 all-gather.18
  483.4 347.2 all-gather.38
  833.7 86.6 all-gather.24
  922.0 143.1 all-gather.28
  1066.6 143.1 all-gather.32
  1211.3 143.2 all-gather.36
  1415.4 178.0 reduce-scatter.30
  1596.2 166.7 reduce-scatter.32
  1765.4 166.7 reduce-scatter.26
  1935.1 133.9 all-gather.40
  2073.0 108.1 reduce-scatter.22
  2185.2 111.2 reduce-scatter.24
  2300.5 110.1 reduce-scatter.28
  2413.6 137.3 reduce-scatter.14
  2553.7 134.2 reduce-scatter.16
  2691.0 354.4 reduce-scatter.20
  3048.5 357.3 reduce-scatter.18
where the time goes:
time: 3420 us; the launch traced here: 3410 us
  waiting for transfers between devices  2580 us (75%)
  blocking collectives  271 us (8%)
  matrix products  253 us (7%)
  local copies, waits for them, and re-layouts  202 us (6%)
  other arithmetic  66 us (2%)
    reduce_scatter x1, waiting for transfers between devices, body(): lax.psum_scatter(value_sum, ('head', 'shard'), scatter_dimension=0, tiled...  360 us
    reduce_scatter x1, waiting for transfers between devices, body(): lax.psum_scatter(project_sum, ('head', 'shard'), scatter_dimension=0, til...  357 us
    all_gather x1, waiting for transfers between devices, carried_in(): everything = jax.tree.map(lambda part: lax.all_gather(part, axis), value)  246 us
    unnamed x24, waiting for transfers between devices  191 us
    dot_general x21, matrix products, product(): return jnp.dot(left, right, preferred_element_type=jnp.float32)  180 us
    reduce_scatter x1, waiting for transfers between devices, body(): lax.psum_scatter(down_whole.astype(jnp.bfloat16), 'head', scatter_dimensi...  161 us
    unnamed x4, blocking collectives  144 us
    all_gather x1, waiting for transfers between devices, body(): lax.all_gather(rows_gate, 'head', axis=1, tiled=True)  138 us
  transfers between devices with their start and end apart: 27, of which 24 were waited for; matrix products, arithmetic and copies ran while one was open for 13% of the time, Pallas kernels for 0%

commit v1 on v0

--- a/solution.py
+++ b/solution.py
@@ -10,6 +10,19 @@
 VD = 128
 EPS_NORM = 1e-05
 HIGH = lax.Precision.HIGHEST
+
+
+def ring_gather(array, axis, dim):
+    size, index, rows = (lax.axis_size(axis), lax.axis_index(axis), array.shape[dim])
+    right = [(i, (i + 1) % size) for i in range(size)]
+    out = jnp.zeros((*array.shape[:dim], size * rows, *array.shape[dim + 1 :]), array.dtype)
+    held = array
+    for step in range(size):
+        holder = (index - step) % size
+        out = lax.dynamic_update_slice_in_dim(out, held, holder * rows, axis=dim)
+        if step < size - 1:
+            held = lax.ppermute(held, axis, right)
+    return out
 
 
 def carried_in(value, axis, combine, identity):
@@ -240,7 +253,7 @@
     full_gate, full_up, full_down = (
         lax.all_gather(rows_gate, "head", axis=1, tiled=True),
         lax.all_gather(rows_up, "head", axis=1, tiled=True),
-        lax.all_gather(rows_down, "head", axis=0, tiled=True),
+        ring_gather(rows_down, "head", 0),
     )
     down_out, grad_active_two, gate_whole, up_whole, down_whole = swiglu_pass(
         active_two, grad_out, full_gate, full_up, full_down

time: 3420 us -> 3300 us (0.965)
  waiting for transfers between devices: 2580 us -> 2440 us
    all_gather x1 -> x0, waiting for transfers between devices: 131 us -> none  [body(): lax.all_gather(rows_down, 'head', axis=0, tiled=True)]
    ppermute x0 -> x3, waiting for transfers between devices: none -> 67.6 us  [ring_gather(): held = lax.ppermute(held, axis, right)]
    all_gather x1, waiting for transfers between devices: 52.3 us -> 0.01 us  [body(): lax.all_gather(query_weight, ('head', 'shard'), axis=0, tiled=True)]
    all_gather x1, waiting for transfers between devices: 246 us -> 195 us  [carried_in(): everything = jax.tree.map(lambda part: lax.all_gather(part, axis), value)]
    unnamed x160 -> x166, local copies, waits for them, and re-layouts: 118 us -> 116 us
    unnamed x24 -> x23, waiting for transfers between devices: 191 us -> 191 us
  transfers between devices with their start and end apart: 27 -> 29, of which waited for: 24 -> 24; matrix products, arithmetic and copies ran while one was open for 13% -> 14% of each run, Pallas kernels for 0% -> 0%
where the time goes in v1:
time: 3300 us; the launch traced here: 3290 us
  waiting for transfers between devices  2440 us (74%)
  matrix products  263 us (8%)
  blocking collectives  258 us (8%)
  local copies, waits for them, and re-layouts  227 us (7%)
  other arithmetic  66 us (2%)
    reduce_scatter x1, waiting for transfers between devices, body(): lax.psum_scatter(value_sum, ('head', 'shard'), scatter_dimension=0, tiled...  360 us
    reduce_scatter x1, waiting for transfers between devices, body(): lax.psum_scatter(project_sum, ('head', 'shard'), scatter_dimension=0, til...  358 us
    all_gather x1, waiting for transfers between devices, carried_in(): everything = jax.tree.map(lambda part: lax.all_gather(part, axis), value)  195 us
    unnamed x23, waiting for transfers between devices  191 us
    dot_general x21, matrix products, product(): return jnp.dot(left, right, preferred_element_type=jnp.float32)  190 us
    reduce_scatter x1, waiting for transfers between devices, body(): lax.psum_scatter(down_whole.astype(jnp.bfloat16), 'head', scatter_dimensi...  161 us
    all_gather x1, waiting for transfers between devices, body(): lax.all_gather(rows_gate, 'head', axis=1, tiled=True)  138 us
    reduce_scatter x1, waiting for transfers between devices, body(): lax.psum_scatter(query_sum, ('head', 'shard'), scatter_dimension=0, tiled...  138 us
  transfers between devices with their start and end apart: 29, of which 24 were waited for; matrix products, arithmetic and copies ran while one was open for 14% of the time, Pallas kernels for 0%

profile of v1, /device:TPU:0, one launch (start us, length us, event | category | flops | bytes accessed | tf_op | source)
XLA Modules:
  0.0 3293.1 jit_solution(14430680303624253717)
XLA Ops:
  12.9 42.1 %all-reduce.7 = (bf16[2048]{0:T(1024)(128)(2,1)S(1)}, bf16[2048]{0:T(1024)(128)(2,1)S(1)}) all-reduce(bf16[2048]{0:T(1024)(128)(2,1)S(1)} %dynamic-update-slice, bf16[2048]{0:T(1024)(128)(2,1)S(1)} %dynamic-update-slice.2), channel_id=1, replica_groups=mesh['head'=4,'shard'=8] {'head','shard'}, use_global_device_ids=true, to_apply=%add | all-reduce | flops 4096 | bytes 16384
  78.9 68.0 %all-gather.22.cloned.1.call-done = bf16[2048,2048]{1,0:T(8,128)(2,1)} async-done(((bf16[64,2048]{1,0:T(8,128)(2,1)}), bf16[2048,2048]{1,0:T(8,128)(2,1)}) %all-gather.22.cloned.1.call-update) | async-done | bytes 8388624 | tf_op jit(solution)/shard_map/all_gather | solution.py:168
  203.1 37.4 %all-gather.26.cloned.1.call-done = bf16[2048,1408]{1,0:T(8,128)(2,1)} async-done(((bf16[256,1408]{1,0:T(8,128)(2,1)}), bf16[2048,1408]{1,0:T(8,128)(2,1)}) %all-gather.26.cloned.1.call-update) | async-done | bytes 5767184 | tf_op jit(solution)/shard_map/all_gather | solution.py:245
  240.5 92.8 %all-gather.30.cloned.1.call-done = bf16[2048,1408]{1,0:T(8,128)(2,1)} async-done(((bf16[256,1408]{1,0:T(8,128)(2,1)}), bf16[2048,1408]{1,0:T(8,128)(2,1)}) %all-gather.30.cloned.1.call-update) | async-done | bytes 5767184 | tf_op jit(solution)/shard_map/all_gather | solution.py:246
  333.4 93.7 %all-gather.34.cloned.1.call-done = bf16[1408,2048]{1,0:T(8,128)(2,1)} async-done(((bf16[1408,256]{1,0:T(8,128)(2,1)}), bf16[1408,2048]{1,0:T(8,128)(2,1)}) %all-gather.34.cloned.1.call-update) | async-done | bytes 5767184 | tf_op jit(solution)/shard_map/all_gather | solution.py:247
  427.0 67.6 %collective-permute-done = bf16[1408,2048]{1,0:T(8,128)(2,1)} collective-permute-done((bf16[1408,2048]{1,0:T(8,128)(2,1)}, bf16[1408,2048]{1,0:T(8,128)(2,1)}, u32[]{:S(2)}, u32[]{:S(2)}) %collective-permute-start) | collective-permute-done | bytes 5767200 | tf_op jit(solution)/shard_map/ppermute | solution.py:24
  503.9 23.9 all-reduce.1
  528.0 32.8 all-to-all-done
  569.6 41.0 %all-gather.2 = f32[32,4,273]{2,1,0:T(4,128)} all-gather(f32[4,4,273]{2,1,0:T(4,128)S(1)} %multiply_reduce_fusion), channel_id=4, replica_groups=mesh['head'=4,'shard'=8] {'shard'}, dimensions={0}, use_global_device_ids=true | all-gather | bytes 157248 | tf_op jit(solution)/shard_map/all_gather | solution.py:30
  636.3 194.9 %all-gather.36.cloned.1.call-done = f32[32,4,273,128]{3,1,2,0:T(4,128)} async-done(((f32[4,4,273,128]{3,1,2,0:T(4,128)}), f32[32,4,273,128]{3,1,2,0:T(4,128)}) %all-gather.36.cloned.1.call-update) | async-done | bytes 17891344 | tf_op jit(solution)/shard_map/all_gather | solution.py:30
  831.2 29.9 while.38
  927.6 138.3 %all-gather.28.cloned.1.call-done = bf16[2048,5632]{1,0:T(8,128)(2,1)} async-done(((bf16[2048,1408]{1,0:T(8,128)(2,1)}), bf16[2048,5632]{1,0:T(8,128)(2,1)}) %all-gather.28.cloned.1.call-update) | async-done | bytes 23068688 | tf_op jit(solution)/shard_map/all_gather | solution.py:254
  1080.3 130.2 %all-gather.32.cloned.1.call-done = bf16[2048,5632]{1,0:T(8,128)(2,1)} async-done(((bf16[2048,1408]{1,0:T(8,128)(2,1)}), bf16[2048,5632]{1,0:T(8,128)(2,1)}) %all-gather.32.cloned.1.call-update) | async-done | bytes 23068688 | tf_op jit(solution)/shard_map/all_gather | solution.py:255
  1223.7 27.6 multiply_convert_fusion
  1264.3 30.7 copy.221
  1295.0 17.6 convolution_convert_fusion.1
  1312.6 30.2 copy.223
  1396.0 29.4 all_to_all.114
  1448.1 25.1 reduce-scatter.31.cloned.1.call-done
  1481.5 161.0 %reduce-scatter.33.cloned.1.call-done = bf16[1408,2048]{1,0:T(8,128)(2,1)} async-done(((bf16[5632,2048]{1,0:T(8,128)(2,1)}), bf16[1408,2048]{1,0:T(8,128)(2,1)}) %reduce-scatter.33.cloned.1.call-update) | async-done | bytes 5767184
  1651.0 160.9 %reduce-scatter.27.cloned.1.call-done = bf16[1408,2048]{1,0:T(8,128)(2,1)} async-done(((bf16[5632,2048]{1,0:T(8,128)(2,1)}), bf16[1408,2048]{1,0:T(8,128)(2,1)}) %reduce-scatter.27.cloned.1.call-update) | async-done | bytes 5767184 | tf_op jit(solution)/shard_map/reduce_scatter | solution.py:268
  1813.6 22.2 all-reduce.3
  1870.9 33.2 %all-gather.5 = bf16[32,4,273]{2,1,0:T(4,128)(2,1)} all-gather(bf16[4,4,273]{2,1,0:T(4,128)(2,1)S(1)} %bitcast.331), channel_id=7, replica_groups=mesh['head'=4,'shard'=8] {'shard'}, dimensions={0}, use_global_device_ids=true | all-gather | bytes 78624 | tf_op jit(solution)/shard_map/all_gather | solution.py:48
  1910.0 38.9 %all-gather.38.cloned.1.call-done = bf16[32,4,273,128]{3,1,2,0:T(4,128)(2,1)} async-done(((bf16[4,4,273,128]{3,1,2,0:T(4,128)(2,1)}), bf16[32,4,273,128]{3,1,2,0:T(4,128)(2,1)}) %all-gather.38.cloned.1.call-update) | async-done | bytes 8945680 | tf_op jit(solution)/shard_map/all_gather | solution.py:48
  1948.8 28.2 while.39
  2084.5 41.6 %all-reduce.6 = (f32[2048]{0:T(1024)S(1)}, f32[2048]{0:T(1024)S(1)}) all-reduce(f32[2048]{0:T(1024)S(1)} %get-tuple-element.499, f32[2048]{0:T(1024)S(1)} %get-tuple-element.497), channel_id=12, replica_groups=mesh['head'=4,'shard'=8] {'head','shard'}, use_global_device_ids=true, to_apply=%region_16.17.clone | all-reduce | flops 4096 | bytes 32768
  2133.1 43.4 %reduce-scatter.25.cloned.1.call-done = bf16[256,1408]{1,0:T(8,128)(2,1)} async-done(((bf16[2048,1408]{1,0:T(8,128)(2,1)}), bf16[256,1408]{1,0:T(8,128)(2,1)}) %reduce-scatter.25.cloned.1.call-update) | async-done | bytes 720912 | tf_op jit(solution)/shard_map/reduce_scatter | solution.py:278
  2178.8 111.8 %reduce-scatter.29.cloned.1.call-done = bf16[1408,256]{1,0:T(8,128)(2,1)} async-done(((bf16[1408,2048]{1,0:T(8,128)(2,1)}), bf16[1408,256]{1,0:T(8,128)(2,1)}) %reduce-scatter.29.cloned.1.call-update) | async-done | bytes 720912 | tf_op jit(solution)/shard_map/reduce_scatter | solution.py:281
  2292.9 137.8 %reduce-scatter.15.cloned.1.call-done = f32[64,256]{1,0:T(8,128)} async-done(((f32[2048,256]{1,0:T(8,128)}), f32[64,256]{1,0:T(8,128)}) %reduce-scatter.15.cloned.1.call-update) | async-done | bytes 65552 | tf_op jit(solution)/shard_map/reduce_scatter | solution.py:341
  2430.7 137.2 %reduce-scatter.17.cloned.1.call-done = f32[64,256]{1,0:T(8,128)} async-done(((f32[2048,256]{1,0:T(8,128)}), f32[64,256]{1,0:T(8,128)}) %reduce-scatter.17.cloned.1.call-update) | async-done | bytes 65552 | tf_op jit(solution)/shard_map/reduce_scatter | solution.py:342
  2567.9 357.9 %reduce-scatter.21.cloned.1.call-done = f32[64,2048]{1,0:T(8,128)} async-done(((f32[2048,2048]{1,0:T(8,128)}), f32[64,2048]{1,0:T(8,128)}) %reduce-scatter.21.cloned.1.call-update) | async-done | bytes 524304 | tf_op jit(solution)/shard_map/reduce_scatter | solution.py:344
  2925.8 360.3 %reduce-scatter.19.cloned.1.call-done = f32[64,2048]{1,0:T(8,128)} async-done(((f32[2048,2048]{1,0:T(8,128)}), f32[64,2048]{1,0:T(8,128)}) %reduce-scatter.19.cloned.1.call-update) | async-done | bytes 524304 | tf_op jit(solution)/shard_map/reduce_scatter | solution.py:343
  (427 shorter events, 546.7 us)
Async XLA Ops:
  7.2 60.4 %all-gather.20.cloned.1.call-start = ((), (), s32[]{:S(2)}) async-start(), calls=%async_computation.19 | async-start | bytes 1081344 | tf_op jit(solution)/shard_map/all_gather | solution.py:167
  7.9 139.1 %all-gather.22.cloned.1.call-start = ((), (), s32[]{:S(2)}) async-start(), calls=%async_computation.20 | async-start | bytes 8650752 | tf_op jit(solution)/shard_map/all_gather | solution.py:168
  8.7 231.8 %all-gather.26.cloned.1.call-start = ((), (), s32[]{:S(2)}) async-start(), calls=%async_computation.22 | async-start | bytes 6488064 | tf_op jit(solution)/shard_map/all_gather | solution.py:245
  9.4 323.9 %all-gather.30.cloned.1.call-start = ((), (), s32[]{:S(2)}) async-start(), calls=%async_computation.24 | async-start | bytes 6488064 | tf_op jit(solution)/shard_map/all_gather | solution.py:246
  10.0 417.0 %all-gather.34.cloned.1.call-start = ((), (), s32[]{:S(2)}) async-start(), calls=%async_computation.26 | async-start | bytes 6488064 | tf_op jit(solution)/shard_map/all_gather | solution.py:247
  10.6 486.5 %all-gather.18.cloned.1.call-start = ((), (), s32[]{:S(2)}) async-start(), calls=%async_computation.18 | async-start | bytes 1081344 | tf_op jit(solution)/shard_map/all_gather | solution.py:166
  70.3 7.9 all-to-all-start.1
  73.8 492.5 %copy-start.51 = (f32[4,256]{1,0:T(4,128)}, f32[4,256]{1,0:T(4,128)S(1)}, u32[]{:S(2)}) copy-start(f32[4,256]{1,0:T(4,128)S(1)} %compare_convert_fusion.3) | copy-start | bytes 12292
  73.8 794.0 %copy-start.57 = (f32[273]{0:T(512)}, f32[273]{0:T(512)S(1)}, u32[]{:S(2)}) copy-start(f32[273]{0:T(512)S(1)} %pad.3.clone) | copy-start | bytes 3280
  78.9 535.1 %copy-start.37 = (bf16[4,256,4,16]{1,3,2,0:T(8,128)(2,1)}, bf16[4,256,4,16]{1,3,2,0:T(8,128)(2,1)S(1)}, u32[]{:S(2)}) copy-start(bf16[4,256,4,16]{1,3,2,0:T(8,128)(2,1)S(1)} %reshape.281) | copy-start | bytes 393220
  159.6 18.8 all-to-all-start.2
  163.9 667.3 %all-gather.36.cloned.1.call-start = ((), (), s32[]{:S(2)}) async-start(), calls=%async_computation.35 | async-start | bytes 20127744 | tf_op jit(solution)/shard_map/all_gather | solution.py:30
  202.3 718.9 %all-gather.24.cloned.1.call-start = ((), (), s32[]{:S(2)}) async-start(), calls=%async_computation.21 | async-start | bytes 8650752 | tf_op jit(solution)/shard_map/all_gather | solution.py:169
  203.0 862.9 %all-gather.28.cloned.1.call-start = ((), (), s32[]{:S(2)}) async-start(), calls=%async_computation.23 | async-start | bytes 28835840 | tf_op jit(solution)/shard_map/all_gather | solution.py:254
  240.5 970.0 %all-gather.32.cloned.1.call-start = ((), (), s32[]{:S(2)}) async-start(), calls=%async_computation.25 | async-start | bytes 28835840 | tf_op jit(solution)/shard_map/all_gather | solution.py:255
  427.0 67.6 %collective-permute-start = (bf16[1408,2048]{1,0:T(8,128)(2,1)}, bf16[1408,2048]{1,0:T(8,128)(2,1)}, u32[]{:S(2)}, u32[]{:S(2)}) collective-permute-start(bf16[1408,2048]{1,0:T(8,128)(2,1)} %all-gather.34.cloned.1.call-done), channel_id=1, source_target_pairs={{0,8},{8,16},{16,24},{24,0},{1,9},{9,17},{17,25},{25,1},{2,10},{10... | collective-permute-start | bytes 17301512 | tf_op jit(solution)/shard_map/ppermute | solution.py:24
  494.6 141.5 %collective-permute-start.1 = (bf16[1408,2048]{1,0:T(8,128)(2,1)}, bf16[1408,2048]{1,0:T(8,128)(2,1)}, u32[]{:S(2)}, u32[]{:S(2)}) collective-permute-start(bf16[1408,2048]{1,0:T(8,128)(2,1)} %collective-permute-done), channel_id=1, source_target_pairs={{0,8},{8,16},{16,24},{24,0},{1,9},{9,17},{17,25},{25,1},{2,10},{10... | collective-permute-start | bytes 17301512 | tf_op jit(solution)/shard_map/ppermute | solution.py:24
  499.8 60.9 %all-to-all-start = ((bf16[4,2,8192]{2,1,0:T(2,128)(2,1)}), bf16[4,2,8192]{2,1,0:T(2,128)(2,1)}, u32[]{:S(2)}, u32[]{:S(2)}) async-start(bf16[4,2,8192]{2,1,0:T(2,128)(2,1)} %reshape.352), calls=%async_computation | async-start | bytes 262144 | tf_op jit(solution)/shard_map/all_to_all | solution.py:200
  636.1 255.8 %collective-permute-start.2 = (bf16[1408,2048]{1,0:T(8,128)(2,1)}, bf16[1408,2048]{1,0:T(8,128)(2,1)}, u32[]{:S(2)}, u32[]{:S(2)}) collective-permute-start(bf16[1408,2048]{1,0:T(8,128)(2,1)} %collective-permute-done.1), channel_id=1, source_target_pairs={{0,8},{8,16},{16,24},{24,0},{1,9},{9,17},{17,25},{25,1},{2,10},{10... | collective-permute-start | bytes 17301512 | tf_op jit(solution)/shard_map/ppermute | solution.py:24
  882.1 27.9 all-to-all-start.3
  885.6 587.6 %reduce-scatter.31.cloned.1.call-start = ((), (), s32[]{:S(2)}) async-start(), calls=%async_computation.37 | async-start | bytes 28835840
  1295.0 347.6 %reduce-scatter.33.cloned.1.call-start = ((), (), s32[]{:S(2)}) async-start(), calls=%async_computation.38 | async-start | bytes 28835840
  1342.8 469.2 %reduce-scatter.27.cloned.1.call-start = ((), (), s32[]{:S(2)}) async-start(), calls=%async_computation.33 | async-start | bytes 28835840 | tf_op jit(solution)/shard_map/reduce_scatter | solution.py:268
  1357.1 591.7 %all-gather.38.cloned.1.call-start = ((), (), s32[]{:S(2)}) async-start(), calls=%async_computation.36 | async-start | bytes 10063872 | tf_op jit(solution)/shard_map/all_gather | solution.py:48
  1448.0 682.7 %reduce-scatter.23.cloned.1.call-start = ((), (), s32[]{:S(2)}) async-start(), calls=%async_computation.31 | async-start | bytes 6488064 | tf_op jit(solution)/shard_map/reduce_scatter | solution.py:275
  1481.5 695.0 %reduce-scatter.25.cloned.1.call-start = ((), (), s32[]{:S(2)}) async-start(), calls=%async_computation.32 | async-start | bytes 6488064 | tf_op jit(solution)/shard_map/reduce_scatter | solution.py:278
  1651.0 639.6 %reduce-scatter.29.cloned.1.call-start = ((), (), s32[]{:S(2)}) async-start(), calls=%async_computation.34 | async-start | bytes 6488064 | tf_op jit(solution)/shard_map/reduce_scatter | solution.py:281
  1860.7 43.4 %all-to-all-start.5 = ((bf16[4,2,8192]{2,1,0:T(2,128)(2,1)}), bf16[4,2,8192]{2,1,0:T(2,128)(2,1)S(1)}, u32[]{:S(2)}, u32[]{:S(2)}) async-start(bf16[4,2,8192]{2,1,0:T(2,128)(2,1)} %reshape.356), calls=%async_computation.5 | async-start | bytes 262144 | tf_op jit(solution)/shard_map/all_to_all | solution.py:324
  1864.1 566.6 %reduce-scatter.15.cloned.1.call-start = ((), (), s32[]{:S(2)}) async-start(), calls=%async_computation.27 | async-start | bytes 2162688 | tf_op jit(solution)/shard_map/reduce_scatter | solution.py:341
  1909.9 658.0 %reduce-scatter.17.cloned.1.call-start = ((), (), s32[]{:S(2)}) async-start(), calls=%async_computation.28 | async-start | bytes 2162688 | tf_op jit(solution)/shard_map/reduce_scatter | solution.py:342
  2005.1 920.7 %reduce-scatter.21.cloned.1.call-start = ((), (), s32[]{:S(2)}) async-start(), calls=%async_computation.30 | async-start | bytes 17301504 | tf_op jit(solution)/shard_map/reduce_scatter | solution.py:344
  2015.2 1270.9 %reduce-scatter.19.cloned.1.call-start = ((), (), s32[]{:S(2)}) async-start(), calls=%async_computation.29 | async-start | bytes 17301504 | tf_op jit(solution)/shard_map/reduce_scatter | solution.py:343
  (65 other events, 2296.6 us)
Sparse Core Ops, SparseCore 0:
  11.0 56.5 all-gather.19
  70.6 76.3 all-gather.21
  149.2 91.2 all-gather.25
  242.5 90.8 all-gather.29
  335.2 91.7 all-gather.33
  429.9 52.4 all-gather.17
  483.9 347.2 all-gather.35
  834.2 86.9 all-gather.23
  922.7 143.0 all-gather.27
  1067.3 143.1 all-gather.31
  1295.1 178.0 reduce-scatter.30
  1475.8 166.7 reduce-scatter.32
  1645.2 166.7 reduce-scatter.26
  1814.8 133.9 all-gather.37
  1952.8 108.2 reduce-scatter.22
  2065.0 111.4 reduce-scatter.24
  2180.4 110.1 reduce-scatter.28
  2293.4 137.2 reduce-scatter.14
  2433.5 134.2 reduce-scatter.16
  2570.7 355.0 reduce-scatter.20
  2928.7 357.3 reduce-scatter.18
